TPU v7x, 256 devices: a whole 4x4x8 slice. The times are simulated.
256 devices in a mesh: rep: 4 (over x), table: 64 (over z, y, core).
Axes of the slice: x: 4, y: 4, z: 8, core: 2. Of those that a mesh axis runs over, the one named last changes fastest.
Arguments:
- cold_table: float32 [65536, 400], P('table'), may hold values from -3 to 3
- cold_state: float32 [65536], P('table'), may hold values from 0.05 to 1
- hot_table: float32 [8192, 400], P('table'), may hold values from -3 to 3
- hot_state: float32 [8192], P('table'), may hold values from 0.05 to 1
- relations: float32 [512, 400], replicated, may hold values from -2.5 to 2.5
- head_owner: int32 [131072, 1], P(('rep', 'table')), may hold values from 0 to 63; in each aligned block of 512 rows (0 to 511, 512 to 1023, ...) at most 16 rows name the same one
- head_row: int32 [131072], P(('rep', 'table')), may hold values from 0 to 1023
- edge_rel: int32 [131072], P(('rep', 'table')), may hold values from 0 to 511
- edge_tail: int32 [131072], P(('rep', 'table')), may hold values from 0 to 8191, as said below
- neg_ids: int32 [4, 512], P('rep', 'table'), may hold values from 0 to 1023
Outputs:
- new_cold_table: float32 [65536, 400], P('table')
- new_cold_state: float32 [65536], P('table')
- new_hot_table: float32 [8192, 400], P('table')
- new_hot_state: float32 [8192], P('table')
Inputs may be any that keep to these rules, and one draw needn't show every extreme that they name: `head_owner`: among the edges of one device (aligned blocks of 512), no owner is named more than 16 times. `neg_ids`: column j names a row of the cold rows of table index j // 8. `edge_tail`: among the edges of one device (aligned blocks of 512), the tails that lie in one aligned block of 128 hot rows are at most 32 distinct rows, and in some such block exactly 32.
All inputs are finite; a program needn't handle non-finite values.
Results may differ from a plain program's by a relative error of at most 0.00045.
The roundings to bfloat16 on the way count: a program that leaves them out, or rounds other values in their place, can miss the bound.
Values may be sent and summed in bfloat16 or wider, within the bound.
No kernel may reach another device: no remote copies, remote signals or barrier semaphores. Data moves between devices by JAX's collectives and lax.ppermute only.
A program may use at most 128 MiB of HBM per device.

v0:
```python
import jax
import jax.numpy as jnp
from jax import lax
from jax.sharding import PartitionSpec as P

learn_rate = 0.5


def with_relation(relation, vector):
    half_width = vector.shape[1] // 2
    v_re, v_im = (vector[:, :half_width], vector[:, half_width:])
    r_re, r_im = (relation[:, :half_width], relation[:, half_width:])
    return jnp.concatenate([v_re * r_re - v_im * r_im, v_re * r_im + v_im * r_re], axis=1)


def against_relation(relation, vector):
    half_width = vector.shape[1] // 2
    v_re, v_im = (vector[:, :half_width], vector[:, half_width:])
    r_re, r_im = (relation[:, :half_width], relation[:, half_width:])
    return jnp.concatenate([r_re * v_re + r_im * v_im, r_re * v_im - r_im * v_re], axis=1)


def edge_terms(head_vec, relation, tail_vec, negatives, live_mask):
    contract = (((1,), (1,)), ((), ()))
    across = (((0,), (0,)), ((), ()))
    head_f = head_vec.astype(jnp.float32)
    tail_f = tail_vec.astype(jnp.float32)
    queries = with_relation(relation, head_f)
    probes = against_relation(relation, tail_f)
    positive = jnp.sum(queries * tail_f, axis=1)
    query_b = queries.astype(jnp.bfloat16)
    probe_b = probes.astype(jnp.bfloat16)
    tail_scores = lax.dot_general(query_b, negatives, contract, preferred_element_type=jnp.float32)
    head_scores = lax.dot_general(probe_b, negatives, contract, preferred_element_type=jnp.float32)
    pos_weight = -jax.nn.sigmoid(-positive) * live_mask
    tail_weight = (jax.nn.sigmoid(tail_scores) * live_mask[:, None]).astype(jnp.bfloat16)
    head_weight = (jax.nn.sigmoid(head_scores) * live_mask[:, None]).astype(jnp.bfloat16)
    tail_mix = jnp.dot(tail_weight, negatives, preferred_element_type=jnp.float32)
    head_mix = jnp.dot(head_weight, negatives, preferred_element_type=jnp.float32)
    head_grad = against_relation(relation, pos_weight[:, None] * tail_f + tail_mix).astype(
        jnp.bfloat16
    )
    tail_grad = with_relation(relation, pos_weight[:, None] * head_f + head_mix)
    neg_grad = lax.dot_general(
        tail_weight, query_b, across, preferred_element_type=jnp.float32
    ) + lax.dot_general(head_weight, probe_b, across, preferred_element_type=jnp.float32)
    return (head_grad, tail_grad, neg_grad)


def adagrad(weights, state, grad):
    new_state = state + jnp.mean(grad * grad, axis=1)
    return (weights - learn_rate * grad / jnp.sqrt(new_state)[:, None], new_state)


def per_device(
    cold_table,
    cold_state,
    hot_table,
    hot_state,
    relations,
    head_owner,
    head_row,
    edge_rel,
    edge_tail,
    neg_ids,
):
    n_table = lax.axis_size("table")
    edge_count = head_row.shape[0]
    capacity = 2 * edge_count // n_table
    slot_total = n_table * capacity
    feature_width = cold_table.shape[1]
    cold_bf = cold_table.astype(jnp.bfloat16)
    hot_bf = hot_table.astype(jnp.bfloat16)
    local_negs = cold_bf[neg_ids[0]]
    hot_all, negatives = (
        lax.all_gather(hot_bf, "table", axis=0, tiled=True),
        lax.all_gather(local_negs, "table", axis=0, tiled=True),
    )
    owners = head_owner[:, 0]
    onehot = (owners[:, None] == jnp.arange(n_table, dtype=jnp.int32)[None, :]).astype(jnp.int32)
    slot_rank = jnp.sum((jnp.cumsum(onehot, axis=0) - onehot) * onehot, axis=1)
    slot_ids = owners * capacity + slot_rank
    cold_grad = jnp.zeros(cold_table.shape, jnp.float32)
    records = jnp.stack([head_row, edge_rel, edge_tail, jnp.ones_like(head_row)])
    packed = jnp.zeros((4, slot_total), jnp.int32).at[:, slot_ids].set(records)
    arrived = lax.all_to_all(
        packed.reshape(4, n_table, capacity), "table", split_axis=1, concat_axis=1, tiled=True
    )
    arrived = arrived.reshape(4, slot_total)
    row_ids, rel_ids, tail_ids, live_ids = (arrived[0], arrived[1], arrived[2], arrived[3])
    tail_live = live_ids.astype(jnp.float32)
    head_grad, tail_grad, neg_grad = edge_terms(
        cold_bf[row_ids], relations[rel_ids], hot_all[tail_ids], negatives, tail_live
    )
    cold_grad = cold_grad.at[row_ids].add(head_grad.astype(jnp.float32))
    hot_grad = jnp.zeros((hot_all.shape[0], feature_width), jnp.float32).at[tail_ids].add(tail_grad)
    hot_share, neg_share = (
        lax.psum_scatter(hot_grad, "table", scatter_dimension=0, tiled=True),
        lax.psum_scatter(neg_grad, "table", scatter_dimension=0, tiled=True),
    )
    cold_grad = cold_grad.at[neg_ids[0]].add(neg_share)
    cold_total, hot_total = lax.psum((cold_grad, hot_share), "rep")
    new_cold_table, new_cold_state = adagrad(cold_table, cold_state, cold_total)
    new_hot_table, new_hot_state = adagrad(hot_table, hot_state, hot_total)
    return (new_cold_table, new_cold_state, new_hot_table, new_hot_state)


def solution(mesh):
    in_specs = (
        P("table", None),
        P("table"),
        P("table", None),
        P("table"),
        P(),
        P(("rep", "table"), None),
        P(("rep", "table")),
        P(("rep", "table")),
        P(("rep", "table")),
        P("rep", "table"),
    )
    out_specs = (P("table", None), P("table"), P("table", None), P("table"))
    return jax.shard_map(
        per_device, mesh=mesh, in_specs=in_specs, out_specs=out_specs, check_vma=False
    )
```

profile of v0, /device:TPU:1, one launch (start us, length us, event | category | flops | bytes accessed | tf_op | source)
XLA Modules:
  0.0 601.2 jit_solution(7032553859578870648)
XLA Ops:
  7.2 1.6 convert_element_type.50
  9.5 1.2 reduce-window.6
  13.5 1.8 scatter_custom_fusion
  16.4 13.1 %all-to-all-start = ((s32[4,64,16]{2,0,1:T(4,128)}), s32[4,64,16]{2,0,1:T(4,128)S(1)}, u32[]{:S(2)}, u32[]{:S(2)}) async-start(s32[4,64,16]{2,0,1:T(4,128)} %copy.55), calls=%async_computation | async-start | bytes 262144 | tf_op jit(solution)/shard_map/all_to_all | solution.py:86
  29.6 1.8 copy.64
  32.9 55.6 %all-gather = bf16[512,400]{1,0:T(8,128)(2,1)} all-gather(bf16[8,400]{1,0:T(8,128)(2,1)S(1)} %gather_fusion.3), channel_id=2, replica_groups=mesh['rep'=4,'table'=64] {'table'}, dimensions={0}, use_global_device_ids=true | all-gather | bytes 416000 | tf_op jit(solution)/shard_map/all_gather | solution.py:77
  88.4 1.5 copy.56
  90.4 5.1 gather_fusion
  95.5 3.0 fusion.24
  98.8 1.5 copy.69
  100.7 5.1 gather_fusion.1
  105.8 1.4 copy.59
  107.2 1.3 convert_element_type.49
  108.6 10.7 %copy.61 = bf16[8192,400]{1,0:T(8,128)(2,1)} copy(bf16[8192,400]{0,1:T(8,128)(2,1)} %all-gather.3.cloned.1.call-done) | data formatting | bytes 13107200 | tf_op jit(solution)/shard_map/all_gather | solution.py:76
  119.3 9.6 %gather_fusion.2 = bf16[1024,400]{1,0:T(8,128)(2,1)} fusion(bf16[8192,400]{1,0:T(8,128)(2,1)} %copy.61, s32[1024]{0:T(1024)S(1)} %broadcast_clamp_fusion), kind=kCustom, calls=%fused_computation.2 | custom fusion | bytes 1642496 | tf_op jit(solution)/shard_map/gather | solution.py:93
  128.8 1.4 copy.62
  130.5 1.2 copy-done.4
  135.3 1.8 multiply_add_fusion.1
  138.2 1.8 multiply_add_fusion
  140.0 1.8 convolution_add_fusion
  141.9 2.5 multiply_subtract_fusion
  144.5 2.0 copy.65
  146.5 14.1 %scatter_custom_fusion.3 = f32[8192,400]{1,0:T(8,128)} fusion(s32[1024]{0:T(1024)S(1)} %bitcast.52, f32[1024,400]{1,0:T(8,128)} %copy.65, f32[]{:T(128)} %constant.10.clone.1), kind=kCustom, calls=%fused_computation.8 | custom fusion | flops 409600 | bytes 13107712 | tf_op jit(solution)/shard_map/scatter-add | solution.py:96
  162.7 1.8 copy.63
  164.5 7.9 %scatter_custom_fusion.1 = f32[1024,400]{1,0:T(8,128)S(1)} fusion(s32[1024]{0:T(1024)S(1)} %bitcast.50, f32[1024,400]{1,0:T(8,128)} %copy.63, f32[]{:T(128)} %constant.10.clone.1), kind=kCustom, calls=%fused_computation.21 | custom fusion | flops 409600 | bytes 1638912 | tf_op jit(solution)/shard_map/scatter-add | solution.py:95
  172.4 151.4 %all-reduce.5.cloned.1.call-done = f32[512,400]{1,0:T(8,128)} async-done(((f32[512,400]{1,0:T(8,128)}), f32[512,400]{1,0:T(8,128)}) %all-reduce.5.cloned.1.call-update) | async-done | bytes 819216
  323.8 1.6 scatter_custom_fusion.2
  325.4 188.0 %reduce-scatter.2.cloned.1.call-done = f32[128,400]{1,0:T(8,128)} async-done(((f32[8192,400]{1,0:T(8,128)}), f32[128,400]{1,0:T(8,128)}) %reduce-scatter.2.cloned.1.call-update) | async-done | bytes 204816 | tf_op jit(solution)/shard_map/reduce_scatter | solution.py:98
  513.6 72.4 %all-reduce.7.cloned.1.call-done = (f32[1024,400]{1,0:T(8,128)}, f32[128,400]{1,0:T(8,128)}) async-done(((f32[1024,400]{1,0:T(8,128)}, f32[128,400]{1,0:T(8,128)}), (f32[1024,400]{1,0:T(8,128)}, f32[128,400]{1,0:T(8,128)})) %all-reduce.7.cloned.1.call-update) | async-done | bytes 1843216 | tf_op jit(solution)/shard_map/psum | solution.py:102
  585.9 2.0 multiply_reduce_fusion
  588.5 1.8 divide_subtract_fusion
  590.3 2.8 copy.67
  (76 shorter events, 15.8 us)
Async XLA Ops:
  7.2 101.4 %all-gather.3.cloned.1.call-start = ((), (), s32[]{:S(2)}) async-start(), calls=%async_computation.2 | async-start | bytes 6656000 | tf_op jit(solution)/shard_map/all_gather | solution.py:76
  16.4 73.5 %all-to-all-start = ((s32[4,64,16]{2,0,1:T(4,128)}), s32[4,64,16]{2,0,1:T(4,128)S(1)}, u32[]{:S(2)}, u32[]{:S(2)}) async-start(s32[4,64,16]{2,0,1:T(4,128)} %copy.55), calls=%async_computation | async-start | bytes 262144 | tf_op jit(solution)/shard_map/all_to_all | solution.py:86
  29.6 294.2 %all-reduce.5.cloned.1.call-start = ((), (), s32[]{:S(2)}) async-start(), calls=%async_computation.4 | async-start | bytes 2097152
  31.5 1.4 copy-start
  31.5 0.7 copy-start.10
  130.3 1.4 copy-start.4
  132.4 1.0 copy-start.5
  141.8 371.6 %reduce-scatter.2.cloned.1.call-start = ((), (), s32[]{:S(2)}) async-start(), calls=%async_computation.3 | async-start | bytes 17039360 | tf_op jit(solution)/shard_map/reduce_scatter | solution.py:98
  160.6 0.7 copy-start.11
  160.7 425.3 %all-reduce.7.cloned.1.call-start = ((), (), s32[]{:S(2)}) async-start(), calls=%async_computation.5 | async-start | bytes 4718592 | tf_op jit(solution)/shard_map/psum | solution.py:102
  172.4 341.0 %copy-start.7 = (f32[128,400]{0,1:T(8,128)S(1)}, f32[128,400]{0,1:T(8,128)}, u32[]{:S(2)}) copy-start(f32[128,400]{0,1:T(8,128)} %param.12) | copy-start | bytes 614404
  325.4 188.0 %copy-start.2 = (f32[1024,400]{1,0:T(8,128)}, f32[1024,400]{1,0:T(8,128)S(1)}, u32[]{:S(2)}) copy-start(f32[1024,400]{1,0:T(8,128)S(1)} %scatter_custom_fusion.2) | copy-start | bytes 4915204
  513.4 74.5 %copy-start.8 = (f32[1024]{0:T(1024)S(1)}, f32[1024]{0:T(1024)}, u32[]{:S(2)}) copy-start(f32[1024]{0:T(1024)} %param.11) | copy-start | bytes 12292
  513.4 75.1 %copy-start.1 = (f32[1024,400]{1,0:T(8,128)S(1)}, f32[1024,400]{1,0:T(8,128)}, u32[]{:S(2)}) copy-start(f32[1024,400]{1,0:T(8,128)} %copy-done) | copy-start | bytes 4915204
  585.9 2.6 copy-start.3
  590.3 2.8 copy-start.6
  590.3 2.9 copy-start.9
Sparse Core Ops, SparseCore 0:
  10.6 86.7 all-gather.2
  142.0 181.7 all-reduce.4
  328.3 185.0 reduce-scatter.1
  515.6 70.2 all-reduce.6
where the time goes:
time: 602 us; the launch traced here: 601 us
  waiting for transfers between devices  412 us (68%)
  local copies, waits for them, and re-layouts  57.3 us (10%)
  blocking collectives  55.6 us (9%)
  other arithmetic  40 us (7%)
  between operations  14.8 us (2%)
  starting transfers between devices  13.3 us (2%)
  matrix products  8.38 us (1%)
    reduce_scatter x1, waiting for transfers between devices, per_device(): lax.psum_scatter(hot_grad, 'table', scatter_dimension=0, tiled=True)  188 us
    unnamed x5, waiting for transfers between devices  151 us
    psum x1, waiting for transfers between devices, per_device(): cold_total, hot_total = lax.psum((cold_grad, hot_share), 'rep')  72.4 us
    all_gather x1, blocking collectives, per_device(): lax.all_gather(local_negs, 'table', axis=0, tiled=True)  55.6 us
    scatter-add x1, other arithmetic, per_device(): jnp.zeros((hot_all.shape[0], feature_width), jnp.float32).at[tail_ids]  14.1 us
    all_to_all x1, starting transfers between devices, per_device(): lax.all_to_all(packed.reshape(4, n_table, capacity), 'table', split_axis=...  13.1 us
    unnamed x32, local copies, waits for them, and re-layouts  12.7 us
  transfers between devices with their start and end apart: 5, of which 3 were waited for; matrix products, arithmetic and copies ran while one was open for 10% of the time, Pallas kernels for 0%

commit v1 on v0

v1 whole, which is shorter than its diff:
```python
import functools
import jax
import jax.numpy as jnp
from jax import lax
from jax.experimental import pallas as pl
from jax.experimental.pallas import tpu as pltpu
from jax.sharding import PartitionSpec as P

learn_rate = 0.5
HEAD_CAP = 16
TAIL_CAP = 32
GROUP = 8
HALF = 256
FULL = 2 * HALF

BF = jnp.bfloat16
F16 = jnp.float16
F32 = jnp.float32
I32 = jnp.int32


def dot(a, b, dims):
    return lax.dot_general(a, b, (dims, ((), ())), preferred_element_type=F32)


MM = ((1,), (0,))
NT = ((1,), (1,))
TN = ((0,), (0,))


def one_hot(ids, count):
    return (ids[:, None] == lax.broadcasted_iota(I32, (1, count), 1)).astype(BF)


def widen(rows):
    half = rows.shape[-1] // 2
    pad = [(0, 0)] * (rows.ndim - 1) + [(0, HALF - half)]
    return jnp.concatenate([jnp.pad(rows[..., :half], pad), jnp.pad(rows[..., half:], pad)], -1)


def narrow(rows, width):
    half = width // 2
    return jnp.concatenate([rows[..., :half], rows[..., HALF : HALF + half]], -1)


def mask_of(shape, ids_row, base=0):
    return (lax.broadcasted_iota(I32, shape, 0) + base == ids_row).astype(BF)


def two_part_dot(mask, x, dims=MM):
    hi = x.astype(BF)
    lo = (x - hi.astype(F32)).astype(BF)
    return dot(mask, hi, dims) + dot(mask, lo, dims)


def power_of(x):
    peak = jnp.max(jnp.abs(x), keepdims=True)
    power = jnp.floor(jnp.log(jnp.maximum(peak, 1e-30)) * 1.4426950408889634)
    return jnp.clip(power, -90.0, 90.0)


def packed(x, power):
    lane = lax.broadcasted_iota(I32, x.shape, x.ndim - 1)
    return jnp.where(lane >= FULL - 8, power, x * jnp.exp2(12.0 - power))


def unpacked(x):
    lane = lax.broadcasted_iota(I32, x.shape, x.ndim - 1)
    scale = jnp.exp2(x[..., FULL - 1 :] - 12.0)
    return jnp.where(lane >= FULL - 8, 0.0, x * scale)


def with_rel(rel, v):
    v_re, v_im, r_re, r_im = v[:, :HALF], v[:, HALF:], rel[:, :HALF], rel[:, HALF:]
    return jnp.concatenate([v_re * r_re - v_im * r_im, v_re * r_im + v_im * r_re], axis=1)


def against_rel(rel, v):
    v_re, v_im, r_re, r_im = v[:, :HALF], v[:, HALF:], rel[:, :HALF], rel[:, HALF:]
    return jnp.concatenate([r_re * v_re + r_im * v_im, r_re * v_im - r_im * v_re], axis=1)


def edge_kernel(
    tail_col, slot_col, slot_row, tail_slot_row, rel_ref, rows_ref, hot_ref, tail_msg, back_msg, acc
):
    step = pl.program_id(0)
    edges = slot_col.shape[0]
    slots = rows_ref.shape[0]
    chunk = hot_ref.shape[0]

    @pl.when(step == 0)
    def _():
        acc[...] = jnp.zeros_like(acc)

    pick = tail_col[...] - step * chunk == lax.broadcasted_iota(I32, (edges, chunk), 1)
    acc[...] += dot(pick.astype(BF), hot_ref[...], MM)

    @pl.when(step == pl.num_programs(0) - 1)
    def _():
        rel = rel_ref[...]
        per = 24
        head_pick = (slot_col[...] == lax.broadcasted_iota(I32, (edges, slots), 1)).astype(BF)
        head_f = dot(head_pick, rows_ref[...], MM)
        n_neg = slots // per * (per - HEAD_CAP)
        j = lax.broadcasted_iota(I32, (n_neg, slots), 0)
        neg_slot = (j >> 3) * per + HEAD_CAP + (j & 7)
        neg_pick = (neg_slot == lax.broadcasted_iota(I32, (n_neg, slots), 1)).astype(BF)
        negatives = dot(neg_pick, rows_ref[...], MM).astype(BF)
        tail_f = acc[...]
        queries = with_rel(rel, head_f)
        probes = against_rel(rel, tail_f)
        positive = jnp.sum(queries * tail_f, axis=1, keepdims=True)
        query_b = queries.astype(BF)
        probe_b = probes.astype(BF)
        pos_weight = -jax.nn.sigmoid(-positive)
        tail_weight = jax.nn.sigmoid(dot(query_b, negatives, NT)).astype(BF)
        head_weight = jax.nn.sigmoid(dot(probe_b, negatives, NT)).astype(BF)
        tail_mix = dot(tail_weight, negatives, MM)
        head_mix = dot(head_weight, negatives, MM)
        head_grad = against_rel(rel, pos_weight * tail_f + tail_mix).astype(BF)
        tail_grad = with_rel(rel, pos_weight * head_f + head_mix)
        neg_grad = dot(tail_weight, query_b, TN) + dot(head_weight, probe_b, TN)

        tail_slots = tail_msg.shape[0]
        sums = two_part_dot(mask_of((tail_slots, edges), tail_slot_row[...]), tail_grad)
        tail_msg[...] = packed(sums, power_of(sums))
        back = dot(mask_of((slots, edges), slot_row[...]), head_grad, MM)
        back = back + two_part_dot(neg_pick, neg_grad, TN)
        back_msg[...] = packed(back, power_of(back))


def edge_call(tail_ids, head_slot, tail_slot, rel, rows, hot_all, tail_slots):
    edges = tail_ids.shape[0]
    slots = rows.shape[0]
    hot = hot_all.shape[0]
    steps = 8
    whole = lambda shape: pl.BlockSpec(shape, lambda i: (0, 0))
    return pl.pallas_call(
        edge_kernel,
        grid=(steps,),
        in_specs=[
            whole((edges, 1)),
            whole((edges, 1)),
            whole((1, edges)),
            whole((1, edges)),
            whole((edges, FULL)),
            whole((slots, FULL)),
            pl.BlockSpec((hot // steps, FULL), lambda i: (i, 0)),
        ],
        out_specs=[whole((tail_slots, FULL)), whole((slots, FULL))],
        out_shape=[
            jax.ShapeDtypeStruct((tail_slots, FULL), F32),
            jax.ShapeDtypeStruct((slots, FULL), F32),
        ],
        scratch_shapes=[pltpu.VMEM((edges, FULL), F32)],
        cost_estimate=pl.CostEstimate(flops=12 << 30, bytes_accessed=24 << 20, transcendentals=1 << 20),
        name="edge",
    )(
        tail_ids[:, None],
        head_slot[:, None],
        head_slot[None, :],
        tail_slot[None, :],
        rel,
        rows,
        hot_all,
    )


def rotated(src, own_ref, msg_ref, me, n_rep):
    own_ref[...] = src(me)
    for k in range(1, n_rep):
        part = src(lax.rem(me + k, n_rep))
        msg_ref[k - 1] = packed(part, power_of(part))


def dense_kernel(me_ref, ids_ref, got_ref, own_ref, msg_ref, dense, *, n_rep):
    near, slots, _ = got_ref.shape
    n_ring, rows, _ = dense.shape
    for z in range(n_ring):
        part = unpacked(got_ref[:, z * TAIL_CAP : (z + 1) * TAIL_CAP, :])
        part = part.reshape(near * TAIL_CAP, FULL)
        mask = mask_of((rows, near * TAIL_CAP), ids_ref[z : z + 1, :])
        dense[z] = two_part_dot(mask, part)
    quarter = rows // n_rep

    def src(q):
        start = pl.multiple_of(q * quarter, quarter)
        return dense[:, pl.ds(start, quarter), :].reshape(n_ring * quarter, FULL)

    rotated(src, own_ref, msg_ref, me_ref[0], n_rep)


def cold_kernel(me_ref, ids_ref, neg_ref, back_ref, own_ref, msg_ref, total, *, n_rep):
    n_src, per, _ = back_ref.shape
    rows = total.shape[0]
    back = unpacked(back_ref[...])
    negs = per - HEAD_CAP
    neg_sum = jnp.sum(back[:, HEAD_CAP:, :], axis=0)
    flat = back.reshape(n_src * per, FULL).astype(BF)
    mask = mask_of((rows, n_src * per), ids_ref[...])
    neg_mask = mask_of((rows, negs), neg_ref[...])
    hi = neg_sum.astype(BF)
    rest = neg_sum - hi.astype(F32)
    total[...] = dot(mask, flat, MM) + dot(neg_mask, hi, MM) + two_part_dot(neg_mask, rest)
    quarter = rows // n_rep

    def src(q):
        return total[pl.ds(pl.multiple_of(q * quarter, quarter), quarter), :]

    rotated(src, own_ref, msg_ref, me_ref[0], n_rep)


def smem():
    return pl.BlockSpec(memory_space=pltpu.SMEM)


def vmem():
    return pl.BlockSpec(memory_space=pltpu.VMEM)


def rotate_call(kernel, name, me, operands, rows, scratch, n_rep):
    return pl.pallas_call(
        functools.partial(kernel, n_rep=n_rep),
        in_specs=[smem()] + [vmem()] * len(operands),
        out_specs=[vmem(), vmem()],
        out_shape=[
            jax.ShapeDtypeStruct((rows, FULL), F32),
            jax.ShapeDtypeStruct((n_rep - 1, rows, FULL), F32),
        ],
        scratch_shapes=[pltpu.VMEM(scratch, F32)],
        cost_estimate=pl.CostEstimate(flops=4 << 30, bytes_accessed=8 << 20, transcendentals=0),
        name=name,
    )(me, *operands)


def shift(x, step, n_rep):
    return lax.ppermute(x, "rep", [(i, (i + step) % n_rep) for i in range(n_rep)])


def sum_kernel(own_ref, got_ref, msg_ref):
    total = own_ref[...]
    for k in range(got_ref.shape[0]):
        total = total + unpacked(got_ref[k])
    msg_ref[...] = packed(total, power_of(total))


def update_kernel(me_ref, table_ref, state_ref, msg_ref, table_out, state_out):
    width = table_ref.shape[1]
    grad = narrow(unpacked(msg_ref[0]), width)
    state = state_ref[...] + jnp.sum(grad * grad, axis=1, keepdims=True) / width
    state_out[...] = state
    table_out[...] = table_ref[...] - learn_rate * grad / jnp.sqrt(state)


def cold_update(me, table, state, msgs, n_rep):
    rows, width = table.shape
    quarter = rows // n_rep
    at = lambda k, me: (lax.rem(me[0] - k + n_rep, n_rep), 0)
    new_table, new_state = pl.pallas_call(
        update_kernel,
        grid_spec=pltpu.PrefetchScalarGridSpec(
            num_scalar_prefetch=1,
            grid=(n_rep,),
            in_specs=[
                pl.BlockSpec((quarter, width), at),
                pl.BlockSpec((quarter, 1), at),
                pl.BlockSpec((1, quarter, FULL), lambda k, me: (k, 0, 0)),
            ],
            out_specs=[pl.BlockSpec((quarter, width), at), pl.BlockSpec((quarter, 1), at)],
        ),
        out_shape=[
            jax.ShapeDtypeStruct((rows, width), F32),
            jax.ShapeDtypeStruct((rows, 1), F32),
        ],
        name="update",
    )(me, table, state[:, None], msgs)
    return new_table, new_state[:, 0]


def adagrad(weights, state, grad):
    new_state = state + jnp.mean(grad * grad, axis=1)
    return (weights - learn_rate * grad / jnp.sqrt(new_state)[:, None], new_state)


def per_device(
    cold_table,
    cold_state,
    hot_table,
    hot_state,
    relations,
    head_owner,
    head_row,
    edge_rel,
    edge_tail,
    neg_ids,
):
    n_table = lax.axis_size("table")
    n_rep = lax.axis_size("rep")
    n_ring = n_table // GROUP
    edges = head_row.shape[0]
    width = cold_table.shape[1]
    cold_rows = cold_table.shape[0]
    hot_rows = hot_table.shape[0]
    negs = neg_ids.shape[1]
    near = [[z * GROUP + g for g in range(GROUP)] for z in range(n_ring)]
    far = [[z * GROUP + g for z in range(n_ring)] for g in range(GROUP)]

    per = HEAD_CAP + negs
    me = lax.axis_index("rep").astype(I32).reshape(1)

    hot_all = lax.all_gather(widen(hot_table.astype(BF)), "table", axis=0, tiled=True)
    cold_bf = widen(cold_table.astype(BF))

    owner_hot = one_hot(head_owner[:, 0], n_table)
    row = lax.broadcasted_iota(jnp.int32, (edges, edges), 0)
    col = lax.broadcasted_iota(jnp.int32, (edges, edges), 1)
    before = dot((col < row).astype(BF), owner_hot, ((1,), (0,)))
    rank = jnp.sum(before * owner_hot.astype(F32), axis=1).astype(jnp.int32)
    head_slot = head_owner[:, 0] * per + rank

    block = edge_tail // hot_rows
    within = edge_tail % hot_rows
    block_hot = one_hot(block, n_table)
    within_hot = one_hot(within, hot_rows)
    present = (dot(block_hot, within_hot, ((0,), (0,))) > 0.5).astype(BF)
    prow = lax.broadcasted_iota(jnp.int32, (hot_rows, hot_rows), 0)
    pcol = lax.broadcasted_iota(jnp.int32, (hot_rows, hot_rows), 1)
    ranks = dot(present, (prow < pcol).astype(BF), ((1,), (0,)))
    rank_of = dot(block_hot, ranks.astype(BF), ((1,), (0,)))
    tail_rank = jnp.sum(rank_of * within_hot.astype(F32), axis=1).astype(jnp.int32)
    z_of, g_of = block // GROUP, block % GROUP
    tail_slot = (g_of * n_ring + z_of) * TAIL_CAP + tail_rank
    slot_iota = lax.broadcasted_iota(jnp.int32, (n_table, hot_rows, TAIL_CAP), 2)
    match = (ranks.astype(jnp.int32)[:, :, None] == slot_iota) & (present > 0.5)[:, :, None]
    row_iota = lax.broadcasted_iota(jnp.int32, (n_table, hot_rows, TAIL_CAP), 1) + 1
    slot_rows = jnp.sum(jnp.where(match, row_iota, 0), axis=1) - 1
    slot_rows = slot_rows.reshape(n_ring, GROUP, TAIL_CAP).transpose(1, 0, 2)

    wanted = jnp.zeros((n_table * per,), I32).at[head_slot].set(head_row).reshape(n_table, per)
    wanted = lax.all_to_all(wanted[:, :HEAD_CAP], "table", 0, 0)
    dense_rows = lax.all_to_all(
        slot_rows.reshape(GROUP, n_ring * TAIL_CAP), "table", 0, 0, axis_index_groups=near
    )
    dense_ids = dense_rows.reshape(GROUP, n_ring, TAIL_CAP).transpose(1, 0, 2)
    dense_ids = dense_ids.reshape(n_ring, GROUP * TAIL_CAP)
    own_negs = jnp.broadcast_to(neg_ids[0][None, :], (n_table, negs))
    asked = jnp.concatenate([wanted, own_negs], axis=1)
    head_ids = jnp.concatenate([wanted, jnp.full((n_table, negs), -1, I32)], axis=1)
    rows = lax.all_to_all(cold_bf[asked], "table", 0, 0)
    relation = widen(relations[edge_rel])
    tail_msg, back_msg = edge_call(
        edge_tail,
        head_slot,
        tail_slot,
        relation,
        rows.reshape(n_table * per, FULL),
        hot_all,
        n_table * TAIL_CAP,
    )

    tail_got = lax.all_to_all(
        tail_msg.astype(F16).reshape(GROUP, n_ring * TAIL_CAP, FULL),
        "table",
        0,
        0,
        axis_index_groups=near,
    )
    back_msg, tail_got = lax.optimization_barrier((back_msg.astype(F16), tail_got))
    back = lax.all_to_all(back_msg.reshape(n_table, per, FULL), "table", 0, 0)

    quarter = hot_rows // n_rep
    hot_own, hot_msg = rotate_call(
        dense_kernel,
        "dense",
        me,
        (dense_ids, tail_got.astype(F32)),
        n_ring * quarter,
        (n_ring, hot_rows, FULL),
        n_rep,
    )
    hot_msg = hot_msg.astype(F16)
    hot_part = hot_own
    for k in range(1, n_rep):
        hot_part = hot_part + unpacked(shift(hot_msg[k - 1], k, n_rep).astype(F32))
    hot_part, back = lax.optimization_barrier((hot_part, back))
    hot_got = lax.all_to_all(
        hot_part.reshape(n_ring, quarter, FULL), "table", 0, 0, axis_index_groups=far
    )
    hot_sum = jnp.sum(hot_got, axis=0)

    cold_own, cold_msg = rotate_call(
        cold_kernel,
        "cold",
        me,
        (head_ids.reshape(1, n_table * per), neg_ids, back.astype(F32)),
        cold_rows // n_rep,
        (cold_rows, FULL),
        n_rep,
    )
    cold_msg = cold_msg.astype(F16)
    cold_got = jnp.stack([shift(cold_msg[k - 1], k, n_rep) for k in range(1, n_rep)])
    cold_part = pl.pallas_call(
        sum_kernel,
        in_specs=[vmem()] * 2,
        out_specs=vmem(),
        out_shape=jax.ShapeDtypeStruct((cold_rows // n_rep, FULL), F32),
        name="sum",
    )(cold_own, cold_got.astype(F32)).astype(F16)
    parts = jnp.stack([cold_part] + [shift(cold_part, k, n_rep) for k in range(1, n_rep)])
    new_cold_table, new_cold_state = cold_update(
        me, cold_table, cold_state, parts.astype(F32), n_rep
    )

    hot_parts = [hot_sum] + [shift(hot_sum, k, n_rep) for k in range(1, n_rep)]
    hot_total = jnp.zeros((n_rep, quarter, FULL), F32)
    for k, part in enumerate(hot_parts):
        hot_total = lax.dynamic_update_index_in_dim(
            hot_total, part, lax.rem(me[0] - k + n_rep, n_rep), 0
        )
    hot_total = narrow(hot_total.reshape(hot_rows, FULL), width)
    new_hot_table, new_hot_state = adagrad(hot_table, hot_state, hot_total)
    return (new_cold_table, new_cold_state, new_hot_table, new_hot_state)


def solution(mesh):
    in_specs = (
        P("table", None),
        P("table"),
        P("table", None),
        P("table"),
        P(),
        P(("rep", "table"), None),
        P(("rep", "table")),
        P(("rep", "table")),
        P(("rep", "table")),
        P("rep", "table"),
    )
    out_specs = (P("table", None), P("table"), P("table", None), P("table"))
    return jax.shard_map(
        per_device, mesh=mesh, in_specs=in_specs, out_specs=out_specs, check_vma=False
    )
```

time: 602 us -> 305 us (0.51)
  waiting for transfers between devices: 412 us -> 134 us
  blocking collectives: 55.6 us -> 0 us
  starting transfers between devices: 13.3 us -> 56.3 us
  Pallas kernels: 0 us -> 41.4 us
  local copies, waits for them, and re-layouts: 57.3 us -> 24.3 us
  other arithmetic: 40 us -> 31.4 us
  matrix products: 8.38 us -> 1.83 us
    reduce_scatter x1 -> x0, waiting for transfers between devices: 188 us -> none  [per_device(): lax.psum_scatter(hot_grad, 'table', scatter_dimension=0, tiled=True)]
    unnamed x5 -> x1, waiting for transfers between devices: 151 us -> 0.02 us
    all_to_all x1 -> x6, waiting for transfers between devices: 0.01 us -> 81.6 us  [the longest x1 40.6 us: per_device(): rows = lax.all_to_all(cold_bf[asked], 'table', 0, 0)]
    psum x1 -> x0, waiting for transfers between devices: 72.4 us -> none  [per_device(): cold_total, hot_total = lax.psum((cold_grad, hot_share), 'rep')]
    all_gather x1 -> x0, blocking collectives: 55.6 us -> none  [per_device(): lax.all_gather(local_negs, 'table', axis=0, tiled=True)]
    pallas_call x0 -> x5, Pallas kernels: none -> 41.4 us  [the longest x1 22.5 us: edge_call(): pl.pallas_call(edge_kernel, grid=(steps,), in_specs=[whole((edges, 1)), w...]
    ppermute x0 -> x12, waiting for transfers between devices: none -> 36.8 us  [shift(): lax.ppermute(x, 'rep', [(i, (i + step) % n_rep) for i in range(n_rep)])]
    all_to_all x1 -> x6, starting transfers between devices: 13.1 us -> 39.3 us  [the longest x1 13.1 us: per_device(): wanted = lax.all_to_all(wanted[:, :HEAD_CAP], 'table', 0, 0)]
  transfers between devices with their start and end apart: 5 -> 19, of which waited for: 3 -> 16; matrix products, arithmetic and copies ran while one was open for 10% -> 16% of each run, Pallas kernels for 0% -> 6%
where the time goes in v1:
time: 305 us; the launch traced here: 304 us
  waiting for transfers between devices  134 us (44%)
  starting transfers between devices  56.3 us (18%)
  Pallas kernels  41.4 us (14%)
  other arithmetic  31.4 us (10%)
  local copies, waits for them, and re-layouts  24.3 us (8%)
  between operations  14.5 us (5%)
    all_to_all x1, waiting for transfers between devices, per_device(): rows = lax.all_to_all(cold_bf[asked], 'table', 0, 0)  40.6 us
    ppermute x12, waiting for transfers between devices, shift(): lax.ppermute(x, 'rep', [(i, (i + step) % n_rep) for i in range(n_rep)])  36.8 us
    all_to_all x1, waiting for transfers between devices, per_device(): lax.all_to_all(tail_msg.astype(F16).reshape(GROUP, n_ring * TAIL_CAP, FUL...  24.3 us
    pallas_call x1, Pallas kernels, edge_call(): pl.pallas_call(edge_kernel, grid=(steps,), in_specs=[whole((edges, 1)), w...  22.5 us
    ppermute x12, starting transfers between devices, shift(): lax.ppermute(x, 'rep', [(i, (i + step) % n_rep) for i in range(n_rep)])  17 us
    all_gather x1, waiting for transfers between devices, per_device(): lax.all_gather(widen(hot_table.astype(BF)), 'table', axis=0, tiled=True)  15.5 us
    all_to_all x1, starting transfers between devices, per_device(): wanted = lax.all_to_all(wanted[:, :HEAD_CAP], 'table', 0, 0)  13.1 us
    pallas_call x2, Pallas kernels, rotate_call(): pl.pallas_call(functools.partial(kernel, n_rep=n_rep), in_specs=[smem()]...  11.1 us
  transfers between devices with their start and end apart: 19, of which 16 were waited for; matrix products, arithmetic and copies ran while one was open for 16% of the time, Pallas kernels for 6%

profile of v1, /device:TPU:1, one launch (start us, length us, event | category | flops | bytes accessed | tf_op | source)
XLA Modules:
  0.0 303.5 jit_solution(844874794155154041)
XLA Ops:
  12.6 2.6 scatter_custom_fusion
  15.9 13.1 %all-to-all-start = ((s32[64,1,16]{2,1,0:T(1,128)}), s32[64,1,16]{2,1,0:T(1,128)S(1)}, u32[]{:S(2)}, u32[]{:S(2)}) async-start(s32[64,1,16]{2,1,0:T(1,128)} %bitcast.5), calls=%async_computation | async-start | bytes 65536 | tf_op jit(solution)/shard_map/all_to_all | solution.py:340
  32.5 6.0 %all-to-all-done = s32[64,1,16]{2,1,0:T(1,128)S(1)} async-done(((s32[64,1,16]{2,1,0:T(1,128)}), s32[64,1,16]{2,1,0:T(1,128)S(1)}, u32[]{:S(2)}, u32[]{:S(2)}) %all-to-all-start) | async-done | bytes 4128 | tf_op jit(solution)/shard_map/all_to_all | solution.py:340
  38.8 5.4 %gather_fusion.1 = bf16[1536,512]{1,0:T(8,128)(2,1)} fusion(bf16[1024,512]{1,0:T(8,128)(2,1)S(1)} %fusion.3, s32[2048]{0:T(1024)S(1)} %pad_clamp_fusion), kind=kCustom, calls=%fused_computation.1 | custom fusion | bytes 3151872 | tf_op jit(solution)/shard_map/gather | solution.py:349
  44.2 5.7 %all-to-all-start.2 = ((bf16[64,24,512]{2,1,0:T(8,128)(2,1)}), bf16[64,24,512]{2,1,0:T(8,128)(2,1)}, u32[]{:S(2)}, u32[]{:S(2)}) async-start(bf16[64,24,512]{2,1,0:T(8,128)(2,1)} %bitcast.15), calls=%async_computation.2 | async-start | bytes 3145728 | tf_op jit(solution)/shard_map/all_to_all | solution.py:349
  56.2 40.6 %all-to-all-done.2 = bf16[64,24,512]{2,1,0:T(8,128)(2,1)} async-done(((bf16[64,24,512]{2,1,0:T(8,128)(2,1)}), bf16[64,24,512]{2,1,0:T(8,128)(2,1)}, u32[]{:S(2)}, u32[]{:S(2)}) %all-to-all-start.2) | async-done | bytes 1572896 | tf_op jit(solution)/shard_map/all_to_all | solution.py:349
  96.8 15.5 %all-gather.2.cloned.1.call-done.hot_ref = bf16[8192,512]{1,0:T(8,128)(2,1)} async-done(((bf16[128,512]{1,0:T(8,128)(2,1)}), bf16[8192,512]{1,0:T(8,128)(2,1)}) %all-gather.2.cloned.1.call-update) | async-done | bytes 8388624 | tf_op jit(solution)/shard_map/all_gather | solution.py:311
  112.3 22.5 %edge.1 = (f32[2048,512]{1,0:T(8,128)}, f32[1536,512]{1,0:T(8,128)}) custom-call(s32[512,1]{1,0:T(8,128)} %copy.76.tail_col, s32[512,1]{1,0:T(8,128)} %get-tuple-element.51.slot_col, s32[1,512]{1,0:T(1,128)} %add.131.slot_row, s32[1,512]{1,0:T(1,128)} %bitcast.76, f32[512,512]{1,0:T(8,128)} %select_maximum_fusion.rel_ref, ...), custom_call_target="tpu_custom_call" | custom-call | flops 12884901888 | bytes 25165824 | tf_op jit(solution)/shard_map/edge/pallas_call | solution.py:138
  134.8 4.0 %convert_element_type.116 = f16[2048,512]{1,0:T(8,128)(2,1)} convert(f32[2048,512]{1,0:T(8,128)} %get-tuple-element.17) | non-fusion elementwise | flops 1048576 | bytes 6291456 | tf_op jit(solution)/shard_map/convert_element_type | solution.py:362
  138.8 4.5 %all-to-all-start.3 = ((f16[8,256,512]{2,1,0:T(8,128)(2,1)}), f16[8,256,512]{2,1,0:T(8,128)(2,1)S(1)}, u32[]{:S(2)}, u32[]{:S(2)}) async-start(f16[8,256,512]{2,1,0:T(8,128)(2,1)} %bitcast.58), calls=%async_computation.3 | async-start | bytes 4194304 | tf_op jit(solution)/shard_map/all_to_all | solution.py:361
  145.1 24.3 %all-to-all-done.3 = f16[8,256,512]{2,1,0:T(8,128)(2,1)S(1)} async-done(((f16[8,256,512]{2,1,0:T(8,128)(2,1)}), f16[8,256,512]{2,1,0:T(8,128)(2,1)S(1)}, u32[]{:S(2)}, u32[]{:S(2)}) %all-to-all-start.3) | async-done | bytes 2097184 | tf_op jit(solution)/shard_map/all_to_all | solution.py:361
  169.5 4.2 %all-to-all-start.1 = ((s32[8,1,256]{2,1,0:T(1,128)}), s32[8,1,256]{2,1,0:T(1,128)S(1)}, u32[]{:S(2)}, u32[]{:S(2)}) async-start(s32[8,1,256]{2,1,0:T(1,128)} %all_to_all.35), calls=%async_computation.1 | async-start | bytes 16384 | tf_op jit(solution)/shard_map/all_to_all | solution.py:341
  173.7 3.4 %convert_element_type.115 = f16[1536,512]{1,0:T(8,128)(2,1)} convert(f32[1536,512]{1,0:T(8,128)} %get-tuple-element.16) | non-fusion elementwise | flops 786432 | bytes 4718592 | tf_op jit(solution)/shard_map/convert_element_type | solution.py:368
  178.3 7.3 %all-to-all-start.4 = ((f16[64,24,512]{2,1,0:T(8,128)(2,1)}), f16[64,24,512]{2,1,0:T(8,128)(2,1)}, u32[]{:S(2)}, u32[]{:S(2)}) async-start(f16[64,24,512]{2,1,0:T(8,128)(2,1)} %bitcast.59), calls=%async_computation.4 | async-start | bytes 3145728 | tf_op jit(solution)/shard_map/all_to_all | solution.py:369
  186.4 2.5 convert_element_type.117.got_ref
  188.9 5.0 %dense.1 = (f32[256,512]{1,0:T(8,128)}, f32[3,256,512]{2,1,0:T(8,128)}) custom-call(s32[1]{0:T(128)} %bitcast.me_ref, s32[8,256]{1,0:T(8,128)} %reshape.196.ids_ref, f32[8,256,512]{2,1,0:T(8,128)} %convert_element_type.117.got_ref), custom_call_target="tpu_custom_call" | custom-call | flops 4294967296 | bytes 8388608 | tf_op jit(solution)/shard_map/dense/pallas_call | solution.py:222
  195.6 2.4 collective-permute-start.2
  200.0 3.8 %collective-permute-done.2 = f16[256,512]{1,0:T(8,128)(2,1)S(1)} collective-permute-done((f16[256,512]{1,0:T(8,128)(2,1)S(1)}, f16[256,512]{1,0:T(8,128)(2,1)S(1)}, u32[]{:S(2)}, u32[]{:S(2)}) %collective-permute-start.2) | collective-permute-done | bytes 262176 | tf_op jit(solution)/shard_map/ppermute | solution.py:237
  203.9 2.9 collective-permute-done.1
  206.8 6.7 %collective-permute-done = f16[256,512]{1,0:T(8,128)(2,1)S(1)} collective-permute-done((f16[256,512]{1,0:T(8,128)(2,1)S(1)}, f16[256,512]{1,0:T(8,128)(2,1)S(1)}, u32[]{:S(2)}, u32[]{:S(2)}) %collective-permute-start) | collective-permute-done | bytes 262176 | tf_op jit(solution)/shard_map/ppermute | solution.py:237
  215.2 9.4 %all-to-all-done.4 = f16[64,24,512]{2,1,0:T(8,128)(2,1)} async-done(((f16[64,24,512]{2,1,0:T(8,128)(2,1)}), f16[64,24,512]{2,1,0:T(8,128)(2,1)}, u32[]{:S(2)}, u32[]{:S(2)}) %all-to-all-start.4) | async-done | bytes 1572896 | tf_op jit(solution)/shard_map/all_to_all | solution.py:369
  224.6 4.5 %all-to-all-start.5 = ((f32[8,32,512]{2,1,0:T(8,128)}), f32[8,32,512]{2,1,0:T(8,128)S(1)}, u32[]{:S(2)}, u32[]{:S(2)}) async-start(f32[8,32,512]{2,1,0:T(8,128)} %bitcast.32), calls=%async_computation.5 | async-start | bytes 1048576 | tf_op jit(solution)/shard_map/all_to_all | solution.py:386
  229.1 3.5 %convert_element_type.122.back_ref = f32[64,24,512]{2,1,0:T(8,128)} convert(f16[64,24,512]{2,1,0:T(8,128)(2,1)} %all-to-all-done.4) | non-fusion elementwise | flops 786432 | bytes 4718592 | tf_op jit(solution)/shard_map/convert_element_type | solution.py:395
  232.6 6.2 %cold.1 = (f32[256,512]{1,0:T(8,128)}, f32[3,256,512]{2,1,0:T(8,128)}) custom-call(s32[1]{0:T(128)} %bitcast.me_ref, s32[1,1536]{1,0:T(1,128)} %reshape.194.ids_ref, s32[1,8]{1,0:T(1,128)} %neg_ref.1, f32[64,24,512]{2,1,0:T(8,128)} %convert_element_type.122.back_ref), custom_call_target="tpu_custom_call" | custom-call | flops 4294967296 | bytes 8388608 | tf_op jit(solution)/shard_map/cold/pallas_call | solution.py:222
  245.3 3.8 %collective-permute-done.3 = f16[256,512]{1,0:T(8,128)(2,1)S(1)} collective-permute-done((f16[256,512]{1,0:T(8,128)(2,1)S(1)}, f16[256,512]{1,0:T(8,128)(2,1)S(1)}, u32[]{:S(2)}, u32[]{:S(2)}) %collective-permute-start.3) | collective-permute-done | bytes 262176 | tf_op jit(solution)/shard_map/ppermute | solution.py:237
  249.1 6.4 %collective-permute-done.4 = f16[256,512]{1,0:T(8,128)(2,1)S(1)} collective-permute-done((f16[256,512]{1,0:T(8,128)(2,1)S(1)}, f16[256,512]{1,0:T(8,128)(2,1)S(1)}, u32[]{:S(2)}, u32[]{:S(2)}) %collective-permute-start.4) | collective-permute-done | bytes 262176 | tf_op jit(solution)/shard_map/ppermute | solution.py:237
  256.9 2.8 sum.1
  262.3 2.7 collective-permute-start.7
  269.3 7.3 %collective-permute-done.7 = f16[256,512]{1,0:T(8,128)(2,1)S(1)} collective-permute-done((f16[256,512]{1,0:T(8,128)(2,1)S(1)}, f16[256,512]{1,0:T(8,128)(2,1)S(1)}, u32[]{:S(2)}, u32[]{:S(2)}) %collective-permute-start.7) | collective-permute-done | bytes 262176 | tf_op jit(solution)/shard_map/ppermute | solution.py:237
  278.2 5.0 %update.1 = (f32[1024,400]{1,0:T(8,128)}, f32[1024,1]{1,0:T(8,128)}) custom-call(s32[1]{0:T(128)} %bitcast.me_ref, f32[1024,400]{1,0:T(8,128)} %copy-done, f32[1024,1]{1,0:T(8,128)} %copy.78.state_ref, f32[4,256,512]{2,1,0:T(8,128)} %maximum_convert_fusion.msg_ref), custom_call_target="tpu_custom_call" | custom-call | tf_op jit(solution)/shard_map/update/pallas_call | solution.py:259
  283.3 2.8 copy.80
  288.6 2.4 collective-permute-start.10
  (115 shorter events, 50.0 us)
Async XLA Ops:
  7.2 105.1 %all-gather.2.cloned.1.call-start = ((), (), s32[]{:S(2)}) async-start(), calls=%async_computation.6 | async-start | bytes 8519680 | tf_op jit(solution)/shard_map/all_gather | solution.py:311
  15.9 22.5 %all-to-all-start = ((s32[64,1,16]{2,1,0:T(1,128)}), s32[64,1,16]{2,1,0:T(1,128)S(1)}, u32[]{:S(2)}, u32[]{:S(2)}) async-start(s32[64,1,16]{2,1,0:T(1,128)} %bitcast.5), calls=%async_computation | async-start | bytes 65536 | tf_op jit(solution)/shard_map/all_to_all | solution.py:340
  30.9 1.3 copy-start
  30.9 1.3 copy-start.5
  31.1 1.3 copy-start.9
  44.2 5.7 %copy-start.1 = (f32[512,400]{0,1:T(8,128)S(1)}, f32[512,400]{0,1:T(8,128)}, u32[]{:S(2)}) copy-start(f32[512,400]{0,1:T(8,128)} %param.14) | copy-start | bytes 2457604
  44.2 6.1 %copy-start.7 = (s32[512]{0:T(512)S(1)}, s32[512]{0:T(512)}, u32[]{:S(2)}) copy-start(s32[512]{0:T(512)} %param.17) | copy-start | bytes 6148
  44.2 52.6 %all-to-all-start.2 = ((bf16[64,24,512]{2,1,0:T(8,128)(2,1)}), bf16[64,24,512]{2,1,0:T(8,128)(2,1)}, u32[]{:S(2)}, u32[]{:S(2)}) async-start(bf16[64,24,512]{2,1,0:T(8,128)(2,1)} %bitcast.15), calls=%async_computation.2 | async-start | bytes 3145728 | tf_op jit(solution)/shard_map/all_to_all | solution.py:349
  50.3 1.8 copy-start.4
  138.8 30.7 %all-to-all-start.3 = ((f16[8,256,512]{2,1,0:T(8,128)(2,1)}), f16[8,256,512]{2,1,0:T(8,128)(2,1)S(1)}, u32[]{:S(2)}, u32[]{:S(2)}) async-start(f16[8,256,512]{2,1,0:T(8,128)(2,1)} %bitcast.58), calls=%async_computation.3 | async-start | bytes 4194304 | tf_op jit(solution)/shard_map/all_to_all | solution.py:361
  169.5 8.8 %all-to-all-start.1 = ((s32[8,1,256]{2,1,0:T(1,128)}), s32[8,1,256]{2,1,0:T(1,128)S(1)}, u32[]{:S(2)}, u32[]{:S(2)}) async-start(s32[8,1,256]{2,1,0:T(1,128)} %all_to_all.35), calls=%async_computation.1 | async-start | bytes 16384 | tf_op jit(solution)/shard_map/all_to_all | solution.py:341
  178.3 46.3 %all-to-all-start.4 = ((f16[64,24,512]{2,1,0:T(8,128)(2,1)}), f16[64,24,512]{2,1,0:T(8,128)(2,1)}, u32[]{:S(2)}, u32[]{:S(2)}) async-start(f16[64,24,512]{2,1,0:T(8,128)(2,1)} %bitcast.59), calls=%async_computation.4 | async-start | bytes 3145728 | tf_op jit(solution)/shard_map/all_to_all | solution.py:369
  195.5 18.7 %copy-start.2 = (f32[256,512]{1,0:T(8,128)S(1)}, f32[256,512]{1,0:T(8,128)}, u32[]{:S(2)}) copy-start(f32[256,512]{1,0:T(8,128)} %get-tuple-element.19) | copy-start | bytes 1572868
  195.6 8.2 %collective-permute-start.2 = (f16[256,512]{1,0:T(8,128)(2,1)S(1)}, f16[256,512]{1,0:T(8,128)(2,1)S(1)}, u32[]{:S(2)}, u32[]{:S(2)}) collective-permute-start(f16[256,512]{1,0:T(8,128)(2,1)S(1)} %get-tuple-element.56), channel_id=1, source_target_pairs={{0,192},{64,0},{128,64},{192,128},{1,193},{65,1},{129,65},{193,129... | collective-permute-start | bytes 786440 | tf_op jit(solution)/shard_map/ppermute | solution.py:237
  198.0 8.7 %collective-permute-start.1 = (f16[256,512]{1,0:T(8,128)(2,1)S(1)}, f16[256,512]{1,0:T(8,128)(2,1)S(1)}, u32[]{:S(2)}, u32[]{:S(2)}) collective-permute-start(f16[256,512]{1,0:T(8,128)(2,1)S(1)} %get-tuple-element.57), channel_id=1, source_target_pairs={{0,128},{64,192},{128,0},{192,64},{1,129},{65,193},{129,1},{193,65... | collective-permute-start | bytes 786440 | tf_op jit(solution)/shard_map/ppermute | solution.py:237
  198.7 14.8 %collective-permute-start = (f16[256,512]{1,0:T(8,128)(2,1)S(1)}, f16[256,512]{1,0:T(8,128)(2,1)S(1)}, u32[]{:S(2)}, u32[]{:S(2)}) collective-permute-start(f16[256,512]{1,0:T(8,128)(2,1)S(1)} %get-tuple-element.55), channel_id=1, source_target_pairs={{0,64},{64,128},{128,192},{192,0},{1,65},{65,129},{129,193},{193,1... | collective-permute-start | bytes 786440 | tf_op jit(solution)/shard_map/ppermute | solution.py:237
  224.6 62.3 %all-to-all-start.5 = ((f32[8,32,512]{2,1,0:T(8,128)}), f32[8,32,512]{2,1,0:T(8,128)S(1)}, u32[]{:S(2)}, u32[]{:S(2)}) async-start(f32[8,32,512]{2,1,0:T(8,128)} %bitcast.32), calls=%async_computation.5 | async-start | bytes 1048576 | tf_op jit(solution)/shard_map/all_to_all | solution.py:386
  240.5 8.6 %collective-permute-start.3 = (f16[256,512]{1,0:T(8,128)(2,1)S(1)}, f16[256,512]{1,0:T(8,128)(2,1)S(1)}, u32[]{:S(2)}, u32[]{:S(2)}) collective-permute-start(f16[256,512]{1,0:T(8,128)(2,1)S(1)} %get-tuple-element.52), channel_id=1, source_target_pairs={{0,64},{64,128},{128,192},{192,0},{1,65},{65,129},{129,193},{193,1... | collective-permute-start | bytes 786440 | tf_op jit(solution)/shard_map/ppermute | solution.py:237
  241.7 13.8 %collective-permute-start.4 = (f16[256,512]{1,0:T(8,128)(2,1)S(1)}, f16[256,512]{1,0:T(8,128)(2,1)S(1)}, u32[]{:S(2)}, u32[]{:S(2)}) collective-permute-start(f16[256,512]{1,0:T(8,128)(2,1)S(1)} %get-tuple-element.54), channel_id=1, source_target_pairs={{0,128},{64,192},{128,0},{192,64},{1,129},{65,193},{129,1},{193,65... | collective-permute-start | bytes 786440 | tf_op jit(solution)/shard_map/ppermute | solution.py:237
  244.0 11.5 %collective-permute-start.5 = (f16[256,512]{1,0:T(8,128)(2,1)S(1)}, f16[256,512]{1,0:T(8,128)(2,1)S(1)}, u32[]{:S(2)}, u32[]{:S(2)}) collective-permute-start(f16[256,512]{1,0:T(8,128)(2,1)S(1)} %get-tuple-element.53), channel_id=1, source_target_pairs={{0,192},{64,0},{128,64},{192,128},{1,193},{65,1},{129,65},{193,129... | collective-permute-start | bytes 786440 | tf_op jit(solution)/shard_map/ppermute | solution.py:237
  256.9 8.3 %copy-start.6 = (f32[1024]{0:T(1024)S(1)}, f32[1024]{0:T(1024)}, u32[]{:S(2)}) copy-start(f32[1024]{0:T(1024)} %param.11) | copy-start | bytes 12292
  260.8 8.5 %collective-permute-start.6 = (f16[256,512]{1,0:T(8,128)(2,1)S(1)}, f16[256,512]{1,0:T(8,128)(2,1)S(1)}, u32[]{:S(2)}, u32[]{:S(2)}) collective-permute-start(f16[256,512]{1,0:T(8,128)(2,1)S(1)} %convert_element_type.125), channel_id=1, source_target_pairs={{0,64},{64,128},{128,192},{192,0},{1,65},{65,129},{129,193},{193,1... | collective-permute-start | bytes 786440 | tf_op jit(solution)/shard_map/ppermute | solution.py:237
  262.3 14.3 %collective-permute-start.7 = (f16[256,512]{1,0:T(8,128)(2,1)S(1)}, f16[256,512]{1,0:T(8,128)(2,1)S(1)}, u32[]{:S(2)}, u32[]{:S(2)}) collective-permute-start(f16[256,512]{1,0:T(8,128)(2,1)S(1)} %convert_element_type.125), channel_id=1, source_target_pairs={{0,128},{64,192},{128,0},{192,64},{1,129},{65,193},{129,1},{193,65... | collective-permute-start | bytes 786440 | tf_op jit(solution)/shard_map/ppermute | solution.py:237
  265.1 11.5 %collective-permute-start.8 = (f16[256,512]{1,0:T(8,128)(2,1)S(1)}, f16[256,512]{1,0:T(8,128)(2,1)S(1)}, u32[]{:S(2)}, u32[]{:S(2)}) collective-permute-start(f16[256,512]{1,0:T(8,128)(2,1)S(1)} %convert_element_type.125), channel_id=1, source_target_pairs={{0,192},{64,0},{128,64},{192,128},{1,193},{65,1},{129,65},{193,129... | collective-permute-start | bytes 786440 | tf_op jit(solution)/shard_map/ppermute | solution.py:237
  283.3 2.8 copy-start.3
  286.1 9.1 %copy-start.8 = (f32[128]{0:T(128)S(1)}, f32[128]{0:T(128)}, u32[]{:S(2)}) copy-start(f32[128]{0:T(128)} %param.13) | copy-start | bytes 1540
  286.9 4.5 %collective-permute-start.9 = (f32[32,512]{1,0:T(8,128)S(1)}, f32[32,512]{1,0:T(8,128)S(1)}, u32[]{:S(2)}, u32[]{:S(2)}) collective-permute-start(f32[32,512]{1,0:T(8,128)S(1)} %reduce_sum.48), channel_id=1, source_target_pairs={{0,64},{64,128},{128,192},{192,0},{1,65},{65,129},{129,193},{193,1... | collective-permute-start | bytes 196616 | tf_op jit(solution)/shard_map/ppermute | solution.py:237
  288.6 5.2 %collective-permute-start.10 = (f32[32,512]{1,0:T(8,128)S(1)}, f32[32,512]{1,0:T(8,128)S(1)}, u32[]{:S(2)}, u32[]{:S(2)}) collective-permute-start(f32[32,512]{1,0:T(8,128)S(1)} %reduce_sum.48), channel_id=1, source_target_pairs={{0,128},{64,192},{128,0},{192,64},{1,129},{65,193},{129,1},{193,65... | collective-permute-start | bytes 196616 | tf_op jit(solution)/shard_map/ppermute | solution.py:237
  290.9 4.1 %collective-permute-start.11 = (f32[32,512]{1,0:T(8,128)S(1)}, f32[32,512]{1,0:T(8,128)S(1)}, u32[]{:S(2)}, u32[]{:S(2)}) collective-permute-start(f32[32,512]{1,0:T(8,128)S(1)} %reduce_sum.48), channel_id=1, source_target_pairs={{0,192},{64,0},{128,64},{192,128},{1,193},{65,1},{129,65},{193,129... | collective-permute-start | bytes 196616 | tf_op jit(solution)/shard_map/ppermute | solution.py:237
Sparse Core Ops, SparseCore 0:
  11.3 100.9 all-gather.1
